TPU v7x, 128 devices: a whole 4x4x4 slice. The times are simulated.
128 devices in a mesh: fsdp: 32 (over y, z, core), dp: 4 (over x).
Axes of the slice: x: 4, y: 4, z: 4, core: 2. Of those that a mesh axis runs over, the one named last changes fastest.
Arguments:
- tokens: bfloat16 [16384, 4096], P(('fsdp', 'dp')), may hold values from -6 to 6
- gain: float32 [4096], replicated, may hold values from 0.5 to 1.5
- tiles: bfloat16 [512, 128, 128], P('fsdp'), may hold values from -0.25 to 0.25
- tile_rows: int32 [512], replicated, may hold values from 0 to 31, as said below
- tile_cols: int32 [512], replicated, may hold values from 0 to 111, as said below
- cotangent: bfloat16 [16384, 14336], P(('fsdp', 'dp')), may hold values from -6 to 6
Outputs:
- projected: bfloat16 [16384, 14336], P(('fsdp', 'dp'))
- token_grad: bfloat16 [16384, 4096], P(('fsdp', 'dp'))
- tile_grad: float32 [512, 128, 128], P('fsdp')
- gain_grad: float32 [4096], replicated
Inputs may be any that keep to these rules, and one draw needn't show every extreme that they name: The pairs (tile_rows[i], tile_cols[i]) are all different. `tile_cols`: pairs with tile_rows as above.
All inputs are finite; a program needn't handle non-finite values.
Results may differ from a plain program's by a relative error of at most 0.0049.
Values may be sent and summed in bfloat16 or wider, within the bound.
No kernel may reach another device: no remote copies, remote signals or barrier semaphores. Data moves between devices by JAX's collectives and lax.ppermute only.
A program may use at most 256 MiB of HBM per device.

v0:
```python
import jax
import jax.numpy as jnp
from jax import lax
from jax.sharding import PartitionSpec as P


def shards(tokens, gain, tiles, tile_rows, tile_cols, cotangent):
    count = tokens.shape[0]
    width = tokens.shape[1]
    tile = tiles.shape[1]
    row_blocks = width // tile
    col_blocks = cotangent.shape[1] // tile
    x32 = tokens.astype(jnp.float32)
    scale = lax.rsqrt(jnp.mean(x32 * x32, axis=-1, keepdims=True) + 1e-05)
    normed = (x32 * scale * gain).astype(jnp.bfloat16)
    xblocks = normed.reshape(count, row_blocks, tile)
    gblocks = cotangent.reshape(count, col_blocks, tile)
    piece = lax.all_gather(tiles, "fsdp", axis=0, tiled=True)
    rows = tile_rows
    cols = tile_cols
    xsel = jnp.take(xblocks, rows, axis=1)
    gsel = jnp.take(gblocks, cols, axis=1)
    forward = jnp.einsum("tkj,kjm->tkm", xsel, piece, preferred_element_type=jnp.float32)
    backward = jnp.einsum("tkm,kjm->tkj", gsel, piece, preferred_element_type=jnp.float32)
    stacked = jnp.stack([forward, backward], axis=0)
    outsum = jnp.zeros((count, col_blocks, tile), jnp.float32).at[:, tile_cols].add(stacked[0])
    back = jnp.zeros((count, row_blocks, tile), jnp.float32).at[:, tile_rows].add(stacked[1])
    projected = outsum.reshape(count, col_blocks * tile).astype(jnp.bfloat16)
    dnormed = back.reshape(count, width)
    gain_grad = lax.psum(jnp.sum(dnormed * x32 * scale, axis=0), ("fsdp", "dp"))
    inner = jnp.mean(x32 * gain * dnormed, axis=-1, keepdims=True)
    token_grad = (scale * gain * dnormed - x32 * scale**3 * inner).astype(jnp.bfloat16)
    group = tiles.shape[0]
    number = tiles.shape[0] * lax.axis_size("fsdp")

    def group_terms(first):
        rows = lax.dynamic_slice_in_dim(tile_rows, first, group, 0)
        cols = lax.dynamic_slice_in_dim(tile_cols, first, group, 0)
        xsel = jnp.take(xblocks, rows, axis=1)
        gsel = jnp.take(gblocks, cols, axis=1)
        return jnp.einsum("tkj,tkm->kjm", xsel, gsel, preferred_element_type=jnp.float32)

    firsts = group * jnp.arange(number // group, dtype=jnp.int32)
    result = lax.map(group_terms, firsts)
    owned = lax.psum_scatter(
        result.reshape(number, tile, tile), "fsdp", scatter_dimension=0, tiled=True
    )
    tile_grad = lax.psum(owned, "dp")
    return (projected, token_grad, tile_grad, gain_grad)


def solution(mesh):
    placed = (
        P(("fsdp", "dp"), None),
        P(),
        P("fsdp", None, None),
        P(),
        P(),
        P(("fsdp", "dp"), None),
    )
    return jax.shard_map(
        shards,
        mesh=mesh,
        in_specs=placed,
        out_specs=(P(("fsdp", "dp"), None), P(("fsdp", "dp"), None), P("fsdp", None, None), P()),
        check_vma=False,
    )
```

profile of v0, /device:TPU:1, one launch (start us, length us, event | category | flops | bytes accessed | tf_op | source)
XLA Modules:
  0.0 814.4 jit_solution(1176212291491571832)
XLA Ops:
  8.0 6.1 copy.35
  14.0 6.0 copy.36
  21.7 16.2 %gather_fusion.3 = bf16[512,128,128]{2,1,0:T(8,128)(2,1)} fusion(bf16[128,112,128]{2,0,1:T(8,128)(2,1)} %copy.36, s32[1024]{0:T(1024)S(1)} %pad_clamp_fusion.2), kind=kCustom, calls=%fused_computation.3 | custom fusion | bytes 33556480 | tf_op jit(solution)/shard_map/jit(_take)/gather | solution.py:22
  38.5 48.0 %all-gather.2.cloned.1.call-done = bf16[512,128,128]{2,1,0:T(8,128)(2,1)} async-done(((bf16[16,128,128]{2,1,0:T(8,128)(2,1)}), bf16[512,128,128]{2,1,0:T(8,128)(2,1)}) %all-gather.2.cloned.1.call-update) | async-done | bytes 16777232 | tf_op jit(solution)/shard_map/all_gather | solution.py:18
  86.5 28.2 %fusion.9 = f32[512,128,128]{2,1,0:T(8,128)} fusion(bf16[512,128,128]{2,1,0:T(8,128)(2,1)} %all-gather.2.cloned.1.call-done, bf16[512,128,128]{2,1,0:T(8,128)(2,1)} %gather_fusion.3, pred[512]{0:T(512)(128)(4,1)S(1)} %compare_and_fusion.2), kind=kOutput, calls=%fused_computation.22 | convolution fusion | flops 2155872256 | bytes 67109376 | tf_op jit(solution)/shard_map/tkm,kjm->tkj/dot_general | solution.py:24
  115.0 66.1 %scatter_fusion.1 = f32[128,32,128]{2,0,1:T(8,128)S(1)} fusion(f32[128,32,128]{2,0,1:T(8,128)S(1)} %broadcast_in_dim.69, s32[512]{0:T(512)S(1)} %compare_select_fusion.2, f32[512,128,128]{2,1,0:T(8,128)} %fusion.9), kind=kCustom, calls=%fused_computation.5 | custom fusion | flops 8388608 | bytes 100665344 | tf_op jit(solution)/shard_map/scatter-add | solution.py:27
  185.5 2.8 fusion.24
  189.0 237.1 %while.10 = (s32[]{:T(128)}, f32[32,16,128,128]{3,2,1,0:T(8,128)}, s32[32]{0:T(128)S(1)}, s32[512]{0:T(512)S(1)}, bf16[128,32,128]{2,0,1:T(8,128)(2,1)S(1)}, /*i...) while((s32[]{:T(128)}, f32[32,16,128,128]{3,2,1,0:T(8,128)}, ...), condition=%wide.region_5.6_spmd, body=%wide.region_4.5_spmd.sunk | while | flops 67635392 | bytes 4203735 | solution.py:44
  191.6 2.7 gather_fusion
  199.0 2.7 gather_fusion
  206.5 2.7 gather_fusion
  213.9 2.7 gather_fusion
  228.7 2.7 gather_fusion
  250.9 2.7 gather_fusion
  317.6 2.7 gather_fusion
  325.0 2.7 gather_fusion
  347.2 2.7 gather_fusion
  354.6 2.7 gather_fusion
  362.0 2.7 gather_fusion
  376.9 2.7 gather_fusion
  391.7 2.7 gather_fusion
  399.1 2.7 gather_fusion
  421.3 2.7 gather_fusion
  426.4 15.0 %gather_fusion.2 = bf16[512,128,128]{2,1,0:T(8,128)(2,1)} fusion(bf16[128,32,128]{2,0,1:T(8,128)(2,1)S(1)} %get-tuple-element.182, s32[1024]{0:T(1024)S(1)} %pad_clamp_fusion.3), kind=kCustom, calls=%fused_computation.2 | custom fusion | bytes 33556480 | tf_op jit(solution)/shard_map/jit(_take)/gather | solution.py:21
  441.3 148.6 %reduce-scatter.2.cloned.1.call-done = f32[16,128,128]{2,1,0:T(8,128)} async-done(((f32[512,128,128]{2,1,0:T(8,128)}), f32[16,128,128]{2,1,0:T(8,128)}) %reduce-scatter.2.cloned.1.call-update) | async-done | bytes 1048592 | tf_op jit(solution)/shard_map/reduce_scatter | solution.py:45
  590.0 24.5 %fusion.11 = f32[512,128,128]{2,1,0:T(8,128)} fusion(bf16[512,128,128]{2,1,0:T(8,128)(2,1)} %all-gather.2.cloned.1.call-done, bf16[512,128,128]{2,1,0:T(8,128)(2,1)} %gather_fusion.2, pred[512]{0:T(512)(128)(4,1)S(1)} %compare_and_fusion.3), kind=kOutput, calls=%fused_computation.24 | convolution fusion | flops 2155872256 | bytes 67109376 | tf_op jit(solution)/shard_map/tkj,kjm->tkm/dot_general | solution.py:23
  614.5 3.8 broadcast_in_dim.64
  618.3 103.4 %scatter_fusion = f32[128,112,128]{2,0,1:T(8,128)} fusion(f32[128,112,128]{2,0,1:T(8,128)} %broadcast_in_dim.64, s32[512]{0:T(512)S(1)} %compare_select_fusion.3, f32[512,128,128]{2,1,0:T(8,128)} %fusion.11), kind=kCustom, calls=%fused_computation.4 | custom fusion | flops 8388608 | bytes 100665344 | tf_op jit(solution)/shard_map/scatter-add | solution.py:26
  721.7 5.8 convert_element_type.17
  727.5 6.1 copy.34
  733.6 6.1 copy.40
  741.0 64.6 %psum.15 = f32[4096]{0:T(1024)} all-reduce(f32[4096]{0:T(1024)S(1)} %get-tuple-element.68), channel_id=1, replica_groups=mesh['fsdp'=32,'dp'=4] {'fsdp','dp'}, use_global_device_ids=true, to_apply=%region_9.10 | all-reduce | flops 4096 | bytes 32768 | tf_op jit(solution)/shard_map/psum | solution.py:30
  (242 shorter events, 145.7 us)
Async XLA Ops:
  7.2 14.5 %copy-start.2 = (s32[512]{0:T(512)S(1)}, s32[512]{0:T(512)}, u32[]{:S(2)}) copy-start(s32[512]{0:T(512)} %param.12) | copy-start | bytes 6148
  7.2 79.4 %all-gather.2.cloned.1.call-start = ((), (), s32[]{:S(2)}) async-start(), calls=%async_computation.1 | async-start | bytes 17301504 | tf_op jit(solution)/shard_map/all_gather | solution.py:18
  7.9 582.1 %reduce-scatter.2.cloned.1.call-start = ((), (), s32[]{:S(2)}) async-start(), calls=%async_computation.2 | async-start | bytes 34603008 | tf_op jit(solution)/shard_map/reduce_scatter | solution.py:45
  21.7 16.8 %copy-start.3 = (s32[512]{0:T(512)S(1)}, s32[512]{0:T(512)}, u32[]{:S(2)}) copy-start(s32[512]{0:T(512)} %param.11) | copy-start | bytes 6148
  115.0 68.0 %copy-start.1 = (f32[4096]{0:T(1024)S(1)}, f32[4096]{0:T(1024)}, u32[]{:S(2)}) copy-start(f32[4096]{0:T(1024)} %param.9) | copy-start | bytes 49156
  426.1 379.5 %all-reduce.2.cloned.1.call-start = ((), (), s32[]{:S(2)}) async-start(), calls=%async_computation.3 | async-start | bytes 2097152 | tf_op jit(solution)/shard_map/psum | solution.py:48
  721.7 18.0 %copy-start = (bf16[128,4096]{0,1:T(8,128)(2,1)S(1)}, bf16[128,4096]{0,1:T(8,128)(2,1)}, u32[]{:S(2)}) copy-start(bf16[128,4096]{0,1:T(8,128)(2,1)} %get-tuple-element.90) | copy-start | bytes 3145732
Sparse Core Ops, SparseCore 0:
  10.3 76.2 all-gather.1
  426.2 163.6 reduce-scatter.1
  592.5 44.0 all-reduce.1
where the time goes:
time: 820 us; the launch traced here: 814 us
  waiting for transfers between devices  197 us (24%)
  local copies, waits for them, and re-layouts  192 us (23%)
  other arithmetic  184 us (22%)
  matrix products  98.3 us (12%)
  blocking collectives  64.6 us (8%)
  loops' own time  63.1 us (8%)
  between operations  13.9 us (2%)
    reduce_scatter x1, waiting for transfers between devices, shards(): lax.psum_scatter(result.reshape(number, tile, tile), 'fsdp', scatter_dime...  149 us
    scatter-add x1, other arithmetic, shards(): jnp.zeros((count, col_blocks, tile), jnp.float32).at[:, tile_cols]  103 us
    gather x32, local copies, waits for them, and re-layouts, group_terms(): gsel = jnp.take(gblocks, cols, axis=1)  85.9 us
    scatter-add x1, other arithmetic, shards(): jnp.zeros((count, row_blocks, tile), jnp.float32).at[:, tile_rows]  66.1 us
    psum x1, blocking collectives, shards(): gain_grad = lax.psum(jnp.sum(dnormed * x32 * scale, axis=0), ('fsdp', 'dp'))  64.6 us
    another operation x1, loops' own time, shards(): result = lax.map(group_terms, firsts)  63.1 us
    all_gather x1, waiting for transfers between devices, shards(): piece = lax.all_gather(tiles, 'fsdp', axis=0, tiled=True)  48 us
    dot_general x32, matrix products, group_terms(): jnp.einsum('tkj,tkm->kjm', xsel, gsel, preferred_element_type=jnp.float32)  45.6 us
  transfers between devices with their start and end apart: 3, of which 2 were waited for; matrix products, arithmetic and copies ran while one was open for 24% of the time, Pallas kernels for 0%

commit v1 on v0

--- a/solution.py
+++ b/solution.py
@@ -27,7 +27,7 @@
     back = jnp.zeros((count, row_blocks, tile), jnp.float32).at[:, tile_rows].add(stacked[1])
     projected = outsum.reshape(count, col_blocks * tile).astype(jnp.bfloat16)
     dnormed = back.reshape(count, width)
-    gain_grad = lax.psum(jnp.sum(dnormed * x32 * scale, axis=0), ("fsdp", "dp"))
+    gain_grad = lax.psum(lax.psum(jnp.sum(dnormed * x32 * scale, axis=0), "dp"), "fsdp")
     inner = jnp.mean(x32 * gain * dnormed, axis=-1, keepdims=True)
     token_grad = (scale * gain * dnormed - x32 * scale**3 * inner).astype(jnp.bfloat16)
     group = tiles.shape[0]

time: 820 us -> 895 us (1.091)
  blocking collectives: 64.6 us -> 136 us
    psum x1 -> x2, blocking collectives: 64.6 us -> 136 us  [the longest x1 123 us: shards(): lax.psum(lax.psum(jnp.sum(dnormed * x32 * scale, axis=0), 'dp'), 'fsdp')]
  transfers between devices with their start and end apart: 3 -> 3, of which waited for: 2 -> 2; matrix products, arithmetic and copies ran while one was open for 24% -> 22% of each run, Pallas kernels for 0% -> 0%
where the time goes in v1:
time: 895 us; the launch traced here: 886 us
  waiting for transfers between devices  197 us (22%)
  local copies, waits for them, and re-layouts  192 us (21%)
  other arithmetic  184 us (21%)
  blocking collectives  136 us (15%)
  matrix products  98.3 us (11%)
  loops' own time  63.1 us (7%)
  between operations  13.9 us (2%)
    reduce_scatter x1, waiting for transfers between devices, shards(): lax.psum_scatter(result.reshape(number, tile, tile), 'fsdp', scatter_dime...  149 us
    psum x1, blocking collectives, shards(): lax.psum(lax.psum(jnp.sum(dnormed * x32 * scale, axis=0), 'dp'), 'fsdp')  123 us
    scatter-add x1, other arithmetic, shards(): jnp.zeros((count, col_blocks, tile), jnp.float32).at[:, tile_cols]  103 us
    gather x32, local copies, waits for them, and re-layouts, group_terms(): gsel = jnp.take(gblocks, cols, axis=1)  85.9 us
    scatter-add x1, other arithmetic, shards(): jnp.zeros((count, row_blocks, tile), jnp.float32).at[:, tile_rows]  66.1 us
    another operation x1, loops' own time, shards(): result = lax.map(group_terms, firsts)  63.1 us
    all_gather x1, waiting for transfers between devices, shards(): piece = lax.all_gather(tiles, 'fsdp', axis=0, tiled=True)  48 us
    dot_general x32, matrix products, group_terms(): jnp.einsum('tkj,tkm->kjm', xsel, gsel, preferred_element_type=jnp.float32)  45.6 us
  transfers between devices with their start and end apart: 3, of which 2 were waited for; matrix products, arithmetic and copies ran while one was open for 22% of the time, Pallas kernels for 0%

profile of v1, /device:TPU:1, one launch (start us, length us, event | category | flops | bytes accessed | tf_op | source)
XLA Modules:
  0.0 885.6 jit_solution(10198446258675211272)
XLA Ops:
  8.0 6.1 copy.35
  14.0 6.0 copy.36
  21.7 16.2 %gather_fusion.3 = bf16[512,128,128]{2,1,0:T(8,128)(2,1)} fusion(bf16[128,112,128]{2,0,1:T(8,128)(2,1)} %copy.36, s32[1024]{0:T(1024)S(1)} %pad_clamp_fusion.2), kind=kCustom, calls=%fused_computation.3 | custom fusion | bytes 33556480 | tf_op jit(solution)/shard_map/jit(_take)/gather | solution.py:22
  38.5 48.0 %all-gather.2.cloned.1.call-done = bf16[512,128,128]{2,1,0:T(8,128)(2,1)} async-done(((bf16[16,128,128]{2,1,0:T(8,128)(2,1)}), bf16[512,128,128]{2,1,0:T(8,128)(2,1)}) %all-gather.2.cloned.1.call-update) | async-done | bytes 16777232 | tf_op jit(solution)/shard_map/all_gather | solution.py:18
  86.5 28.2 %fusion.9 = f32[512,128,128]{2,1,0:T(8,128)} fusion(bf16[512,128,128]{2,1,0:T(8,128)(2,1)} %all-gather.2.cloned.1.call-done, bf16[512,128,128]{2,1,0:T(8,128)(2,1)} %gather_fusion.3, pred[512]{0:T(512)(128)(4,1)S(1)} %compare_and_fusion.2), kind=kOutput, calls=%fused_computation.22 | convolution fusion | flops 2155872256 | bytes 67109376 | tf_op jit(solution)/shard_map/tkm,kjm->tkj/dot_general | solution.py:24
  115.0 66.1 %scatter_fusion.1 = f32[128,32,128]{2,0,1:T(8,128)S(1)} fusion(f32[128,32,128]{2,0,1:T(8,128)S(1)} %broadcast_in_dim.69, s32[512]{0:T(512)S(1)} %compare_select_fusion.2, f32[512,128,128]{2,1,0:T(8,128)} %fusion.9), kind=kCustom, calls=%fused_computation.5 | custom fusion | flops 8388608 | bytes 100665344 | tf_op jit(solution)/shard_map/scatter-add | solution.py:27
  185.5 2.8 fusion.24
  189.0 237.1 %while.10 = (s32[]{:T(128)}, f32[32,16,128,128]{3,2,1,0:T(8,128)}, s32[32]{0:T(128)S(1)}, s32[512]{0:T(512)S(1)}, bf16[128,32,128]{2,0,1:T(8,128)(2,1)S(1)}, /*i...) while((s32[]{:T(128)}, f32[32,16,128,128]{3,2,1,0:T(8,128)}, ...), condition=%wide.region_5.6_spmd, body=%wide.region_4.5_spmd.sunk | while | flops 67635392 | bytes 4203735 | solution.py:44
  191.6 2.7 gather_fusion
  199.0 2.7 gather_fusion
  213.9 2.7 gather_fusion
  228.7 2.7 gather_fusion
  250.9 2.7 gather_fusion
  317.6 2.7 gather_fusion
  325.0 2.7 gather_fusion
  347.2 2.7 gather_fusion
  354.6 2.7 gather_fusion
  362.0 2.7 gather_fusion
  376.9 2.7 gather_fusion
  391.7 2.7 gather_fusion
  399.1 2.7 gather_fusion
  421.3 2.7 gather_fusion
  426.4 15.0 %gather_fusion.2 = bf16[512,128,128]{2,1,0:T(8,128)(2,1)} fusion(bf16[128,32,128]{2,0,1:T(8,128)(2,1)S(1)} %get-tuple-element.182, s32[1024]{0:T(1024)S(1)} %pad_clamp_fusion.3), kind=kCustom, calls=%fused_computation.2 | custom fusion | bytes 33556480 | tf_op jit(solution)/shard_map/jit(_take)/gather | solution.py:21
  441.3 148.6 %reduce-scatter.2.cloned.1.call-done = f32[16,128,128]{2,1,0:T(8,128)} async-done(((f32[512,128,128]{2,1,0:T(8,128)}), f32[16,128,128]{2,1,0:T(8,128)}) %reduce-scatter.2.cloned.1.call-update) | async-done | bytes 1048592 | tf_op jit(solution)/shard_map/reduce_scatter | solution.py:45
  590.0 24.5 %fusion.11 = f32[512,128,128]{2,1,0:T(8,128)} fusion(bf16[512,128,128]{2,1,0:T(8,128)(2,1)} %all-gather.2.cloned.1.call-done, bf16[512,128,128]{2,1,0:T(8,128)(2,1)} %gather_fusion.2, pred[512]{0:T(512)(128)(4,1)S(1)} %compare_and_fusion.3), kind=kOutput, calls=%fused_computation.24 | convolution fusion | flops 2155872256 | bytes 67109376 | tf_op jit(solution)/shard_map/tkj,kjm->tkm/dot_general | solution.py:23
  614.5 3.8 broadcast_in_dim.64
  618.3 103.4 %scatter_fusion = f32[128,112,128]{2,0,1:T(8,128)} fusion(f32[128,112,128]{2,0,1:T(8,128)} %broadcast_in_dim.64, s32[512]{0:T(512)S(1)} %compare_select_fusion.3, f32[512,128,128]{2,1,0:T(8,128)} %fusion.11), kind=kCustom, calls=%fused_computation.4 | custom fusion | flops 8388608 | bytes 100665344 | tf_op jit(solution)/shard_map/scatter-add | solution.py:26
  721.7 5.8 convert_element_type.17
  727.5 6.1 copy.34
  733.6 6.1 copy.40
  741.0 12.9 %psum.22 = f32[4096]{0:T(1024)S(1)} all-reduce(f32[4096]{0:T(1024)S(1)} %get-tuple-element.68), channel_id=1, replica_groups=mesh['fsdp'=32,'dp'=4] {'dp'}, use_global_device_ids=true, to_apply=%region_9.10 | all-reduce | flops 4096 | bytes 32768 | tf_op jit(solution)/shard_map/psum | solution.py:30
  753.9 122.9 %psum.23 = f32[4096]{0:T(1024)} all-reduce(f32[4096]{0:T(1024)S(1)} %psum.22), channel_id=1, replica_groups=mesh['fsdp'=32,'dp'=4] {'fsdp'}, use_global_device_ids=true, to_apply=%region_10.11 | all-reduce | flops 4096 | bytes 32768 | tf_op jit(solution)/shard_map/psum | solution.py:30
  (243 shorter events, 148.4 us)
Async XLA Ops:
  7.2 14.5 %copy-start.2 = (s32[512]{0:T(512)S(1)}, s32[512]{0:T(512)}, u32[]{:S(2)}) copy-start(s32[512]{0:T(512)} %param.12) | copy-start | bytes 6148
  7.2 79.4 %all-gather.2.cloned.1.call-start = ((), (), s32[]{:S(2)}) async-start(), calls=%async_computation.1 | async-start | bytes 17301504 | tf_op jit(solution)/shard_map/all_gather | solution.py:18
  7.9 582.1 %reduce-scatter.2.cloned.1.call-start = ((), (), s32[]{:S(2)}) async-start(), calls=%async_computation.2 | async-start | bytes 34603008 | tf_op jit(solution)/shard_map/reduce_scatter | solution.py:45
  21.7 16.8 %copy-start.3 = (s32[512]{0:T(512)S(1)}, s32[512]{0:T(512)}, u32[]{:S(2)}) copy-start(s32[512]{0:T(512)} %param.11) | copy-start | bytes 6148
  115.0 68.0 %copy-start.1 = (f32[4096]{0:T(1024)S(1)}, f32[4096]{0:T(1024)}, u32[]{:S(2)}) copy-start(f32[4096]{0:T(1024)} %param.9) | copy-start | bytes 49156
  426.1 450.7 %all-reduce.2.cloned.1.call-start = ((), (), s32[]{:S(2)}) async-start(), calls=%async_computation.3 | async-start | bytes 2097152 | tf_op jit(solution)/shard_map/psum | solution.py:48
  721.7 18.0 %copy-start = (bf16[128,4096]{0,1:T(8,128)(2,1)S(1)}, bf16[128,4096]{0,1:T(8,128)(2,1)}, u32[]{:S(2)}) copy-start(bf16[128,4096]{0,1:T(8,128)(2,1)} %get-tuple-element.90) | copy-start | bytes 3145732
Sparse Core Ops, SparseCore 0:
  10.3 76.2 all-gather.1
  426.2 163.6 reduce-scatter.1
  592.5 44.0 all-reduce.1
